TPU v7x, 1024 devices: a whole 4x4x32 slice. The times are simulated.
1024 devices in a mesh: span: 8 (over x, core), seq: 32 (over z), mp: 4 (over y).
Axes of the slice: x: 4, y: 4, z: 32, core: 2. Of those that a mesh axis runs over, the one named last changes fastest.
Arguments:
- queries: bfloat16 [8, 2048, 3072], P('span', 'seq', 'mp'), may hold values from -256 to 256
- keys_values: bfloat16 [2, 8, 2048, 512], P(None, 'span', 'seq', 'mp'), may hold values from -200 to 200
- clip_tokens: int32 [8], replicated, may hold values from 512 to 2048, as said below
- noise_level: int32 [8], replicated, may hold values from 0 to 63
- level_gate: bfloat16 [64, 3072], P(None, 'mp'), may hold values from -3 to 3
- out_gain: bfloat16 [3072], P('mp'), may hold values from 0.099609375 to 1.8984375
Outputs:
- layer_out: bfloat16 [8, 2048, 3072], P('span', 'seq', 'mp')
Inputs may be any that keep to these rules, and one draw needn't show every extreme that they name: `clip_tokens`: each clip's live slots are its first ones; some clip fills all 2048 slots.
All inputs are finite; a program needn't handle non-finite values.
Results may differ from a plain program's by a relative error of at most 0.0065.
Values may be sent and summed in bfloat16 or wider, within the bound.
A program may use at most 32 MiB of HBM per device.

v0:
```python
import math

import jax
import jax.numpy as jnp
from jax import lax
from jax.sharding import PartitionSpec as P

HEADS = 24
KVH = 4
HD = 128


def per_device(queries, keys_values, clip_tokens, noise_level, level_gate, out_gain):
    tokens_here = queries.shape[1]
    slot_count = tokens_here * lax.axis_size("seq")
    clip_count = clip_tokens.shape[0]
    kv_heads_here = keys_values.shape[-1] // HD
    group_size = HEADS // KVH
    own_clip = lax.axis_index("span")
    own_seq = lax.axis_index("seq")
    query_heads = queries[0].reshape(tokens_here, kv_heads_here, group_size, HD)
    score_scale = 1.0 / math.sqrt(HD)
    clip_ids = jnp.arange(clip_count, dtype=jnp.int32)

    def clip_length(which):
        return jnp.sum(
            jnp.where(which[:, None] == clip_ids[None, :], clip_tokens[None, :], 0), axis=1
        )

    def block_step(running, key_block, first):
        key_count = key_block.shape[1]
        positions = first + jnp.arange(key_count, dtype=jnp.int32)
        holder = positions // slot_count
        slot_index = positions - holder * slot_count
        usable = (holder >= 0) & (holder <= own_clip) & (slot_index < clip_length(holder))

        def update(state):
            running_max, weight_sum, weighted = state
            key_rows = key_block[0].reshape(key_count, kv_heads_here, HD)
            value_rows = key_block[1].reshape(key_count, kv_heads_here, HD)
            scores = (
                jnp.einsum(
                    "tgrd,kgd->tgrk", query_heads, key_rows, preferred_element_type=jnp.float32
                )
                * score_scale
            )
            scores = jnp.where(usable[None, None, None, :], scores, -jnp.inf)
            new_max = jnp.maximum(running_max, jnp.max(scores, axis=-1))
            weights = jnp.exp(scores - new_max[..., None])
            shrink = jnp.exp(running_max - new_max)
            weight_sum = weight_sum * shrink + jnp.sum(weights, axis=-1)
            weighted = weighted * shrink[..., None] + jnp.einsum(
                "tgrk,kgd->tgrd",
                weights.astype(jnp.bfloat16),
                value_rows,
                preferred_element_type=jnp.float32,
            )
            return (new_max, weight_sum, weighted)

        def unchanged(state):
            return state

        return lax.cond(jnp.any(usable), update, unchanged, running)

    initial = (
        jnp.full((tokens_here, kv_heads_here, group_size), -jnp.inf, jnp.float32),
        jnp.zeros((tokens_here, kv_heads_here, group_size), jnp.float32),
        jnp.zeros((tokens_here, kv_heads_here, group_size, HD), jnp.float32),
    )
    local_kv = keys_values[:, 0]
    kv_piece = lax.all_gather(local_kv, ("span", "seq"), axis=1, tiled=True)
    key_count = kv_piece.shape[1]

    def loop_step(block_index, state):
        key_block = lax.dynamic_slice_in_dim(kv_piece, block_index * 1024, 1024, 1)
        return block_step(state, key_block, block_index * 1024)

    running = lax.fori_loop(0, key_count // 1024, loop_step, initial)
    running_max, weight_sum, weighted = running
    attended = (weighted / weight_sum[..., None]).reshape(
        tokens_here, kv_heads_here * group_size * HD
    )
    squares = jnp.sum(attended * attended, axis=1)
    mean_square = lax.psum(squares, "mp") / (HEADS * HD)
    own_level = jnp.sum(jnp.where(clip_ids == own_clip, noise_level, 0))
    one_hot = (jnp.arange(level_gate.shape[0], dtype=jnp.int32) == own_level).astype(jnp.bfloat16)
    gate_row = jnp.dot(one_hot, level_gate, preferred_element_type=jnp.float32)
    own_length = jnp.sum(jnp.where(clip_ids == own_clip, clip_tokens, 0))
    usable_rows = own_seq * tokens_here + jnp.arange(tokens_here, dtype=jnp.int32) < own_length
    normed = (
        attended
        * lax.rsqrt(mean_square + 1e-06)[:, None]
        * out_gain.astype(jnp.float32)
        * (1.0 + gate_row)
    )
    return jnp.where(usable_rows[:, None], normed, 0.0).astype(jnp.bfloat16)[None]


def solution(mesh):
    placed = (
        P("span", "seq", "mp"),
        P(None, "span", "seq", "mp"),
        P(),
        P(),
        P(None, "mp"),
        P("mp"),
    )
    return jax.shard_map(
        per_device, mesh=mesh, in_specs=placed, out_specs=P("span", "seq", "mp"), check_vma=False
    )
```

profile of v0, /device:TPU:6, one launch (start us, length us, event | category | flops | bytes accessed | tf_op | source)
XLA Modules:
  0.0 383.7 jit_solution(2659802779091971849)
XLA Ops:
  13.0 279.2 %all-gather.3.cloned.1.call-done = bf16[2,1,16384,128]{3,2,0,1:T(8,128)(2,1)} async-done(((bf16[2,1,64,128]{3,2,0,1:T(8,128)(2,1)}), bf16[2,1,16384,128]{3,2,0,1:T(8,128)(2,1)}) %all-gather.3.cloned.1.call-update) | async-done | bytes 8388624 | tf_op jit(solution)/shard_map/all_gather | solution.py:71
  292.3 72.9 %while.20 = (s32[]{:T(128)}, f32[64,1,6]{0,2,1:T(8,128)S(1)}, f32[64,1,6]{0,2,1:T(8,128)S(1)}, f32[64,1,6,128]{3,0,2,1:T(8,128)S(1)}, s32[]{:T(128)}, /*index=5*...) while((s32[]{:T(128)}, f32[64,1,6]{0,2,1:T(8,128)S(1)}, ...), condition=%wide.region_8.9_spmd.clone, body=%wide.region_1.8_spmd.clone.sunk | while | flops 204243072 | bytes 5777741 | solution.py:78
  294.4 3.3 conditional.3
  301.8 3.3 conditional.3
  307.2 3.3 conditional.3
  308.6 1.5 fusion.5
  312.6 3.3 conditional.3
  314.0 1.5 fusion.5
  320.0 3.3 conditional.3
  325.4 3.3 conditional.3
  326.9 1.5 fusion.5
  330.8 3.3 conditional.3
  332.2 1.5 fusion.5
  336.2 3.3 conditional.3
  337.6 1.5 fusion.5
  341.6 3.3 conditional.3
  343.0 1.5 fusion.5
  346.9 3.3 conditional.3
  348.4 1.5 fusion.5
  352.3 3.3 conditional.3
  353.8 1.5 fusion.5
  357.7 3.3 conditional.3
  359.1 1.5 fusion.5
  365.6 10.5 %psum.7 = f32[64]{0:T(128)S(1)} all-reduce(f32[64]{0:T(128)S(1)} %get-tuple-element.361), channel_id=1, replica_groups=mesh['span'=8,'seq'=32,'mp'=4] {'mp'}, use_global_device_ids=true, to_apply=%region_10.11 | all-reduce | flops 64 | bytes 512 | tf_op jit(solution)/shard_map/psum | solution.py:84
  (135 shorter events, 55.9 us)
Async XLA Ops:
  6.5 5.7 %copy-start = (bf16[64,768]{1,0:T(8,128)(2,1)S(1)}, bf16[64,768]{1,0:T(8,128)(2,1)}, u32[]{:S(2)}) copy-start(bf16[64,768]{1,0:T(8,128)(2,1)} %param.14) | copy-start | bytes 294916
  6.5 285.7 %all-gather.3.cloned.1.call-start = ((), (), s32[]{:S(2)}) async-start(), calls=%async_computation | async-start | bytes 8421376 | tf_op jit(solution)/shard_map/all_gather | solution.py:71
Sparse Core Ops, SparseCore 0:
  11.6 280.6 all-gather.2
where the time goes:
time: 388 us; the launch traced here: 384 us
  waiting for transfers between devices  280 us (72%)
  matrix products  35.3 us (9%)
  other arithmetic  31.9 us (8%)
  between operations  13.5 us (3%)
  loops' own time  11.3 us (3%)
  blocking collectives  10.5 us (3%)
    all_gather x1, waiting for transfers between devices, per_device(): kv_piece = lax.all_gather(local_kv, ('span', 'seq'), axis=1, tiled=True)  279 us
    dot_general x12, matrix products, update(): jnp.einsum('tgrk,kgd->tgrd', weights.astype(jnp.bfloat16), value_rows, pr...  17.7 us
    dot_general x12, matrix products, update(): jnp.einsum('tgrd,kgd->tgrk', query_heads, key_rows, preferred_element_typ...  16.8 us
    reduce_sum x16, other arithmetic, clip_length(): jnp.sum(jnp.where(which[:, None] == clip_ids[None, :], clip_tokens[None,...  11.8 us
    another operation x1, loops' own time, per_device(): running = lax.fori_loop(0, key_count // 1024, loop_step, initial)  10.6 us
    psum x1, blocking collectives, per_device(): mean_square = lax.psum(squares, 'mp') / (HEADS * HD)  10.5 us
    reduce_or x16, other arithmetic, block_step(): return lax.cond(jnp.any(usable), update, unchanged, running)  10.5 us
  transfers between devices with their start and end apart: 1, of which 1 were waited for; matrix products, arithmetic and copies ran while one was open for 1% of the time, Pallas kernels for 0%

commit v1 on v0

v1 whole, which is shorter than its diff:
```python
import functools
import math

import jax
import jax.numpy as jnp
from jax import lax
from jax.experimental import pallas as pl
from jax.experimental.pallas import tpu as pltpu
from jax.sharding import PartitionSpec as P

HEADS = 24
KVH = 4
HD = 128
GROUP = HEADS // KVH
TOK = 64
NX = 4
NZ = 32
NY = 4
ROWS = GROUP * TOK
EXP_SCALE = math.log2(math.e) / math.sqrt(HD)
LOW = -1e30
MESH = pl.DeviceIdType.MESH


def kernel(
    tok_ref, noise_ref, q_ref, kv_ref, gate_ref, gain_ref, out_ref,
    kvbuf, vtbuf, qbuf, acc, stat, obuf, sbuf, orecv, srecv, sqsend, sqrecv,
    z_send, z_recv, c_send, c_recv, q_send, q_recv, o_send, o_recv, s_send, s_recv, y_send, y_recv,
):
    span = lax.axis_index("span")
    z = lax.axis_index("seq")
    y = lax.axis_index("mp")
    x = span // 2
    core = span % 2
    sibling = span + 1 - 2 * core

    def along_z(step):
        return {"seq": (z + step + NZ) % NZ}

    def z_copy(src, dst_slot, step):
        return pltpu.make_async_remote_copy(
            src_ref=src, dst_ref=kvbuf.at[0, dst_slot],
            send_sem=z_send.at[dst_slot], recv_sem=z_recv.at[dst_slot],
            device_id=along_z(step), device_id_type=MESH,
        )

    def c_copy(src, slot):
        return pltpu.make_async_remote_copy(
            src_ref=src, dst_ref=kvbuf.at[1, slot],
            send_sem=c_send.at[slot], recv_sem=c_recv.at[slot],
            device_id={"span": sibling}, device_id_type=MESH,
        )

    def q_copy(d):
        return pltpu.make_async_remote_copy(
            src_ref=q_ref, dst_ref=qbuf.at[d],
            send_sem=q_send.at[d], recv_sem=q_recv.at[d],
            device_id={"span": (span - 2 * d + 8) % 8}, device_id_type=MESH,
        )

    def o_copy(d):
        return pltpu.make_async_remote_copy(
            src_ref=obuf.at[d], dst_ref=orecv.at[d],
            send_sem=o_send.at[d], recv_sem=o_recv.at[d],
            device_id={"span": (span + 2 * d) % 8}, device_id_type=MESH,
        )

    def s_copy(d):
        return pltpu.make_async_remote_copy(
            src_ref=sbuf.at[d], dst_ref=srecv.at[d],
            send_sem=s_send.at[d], recv_sem=s_recv.at[d],
            device_id={"span": (span + 2 * d) % 8}, device_id_type=MESH,
        )

    def y_copy(d):
        return pltpu.make_async_remote_copy(
            src_ref=sqsend, dst_ref=sqrecv.at[d],
            send_sem=y_send.at[d], recv_sem=y_recv.at[d],
            device_id={"mp": (y + d) % NY}, device_id_type=MESH,
        )

    barrier = pltpu.get_barrier_semaphore()
    for step in (1, -1, 3, -3):
        pl.semaphore_signal(barrier, inc=1, device_id=along_z(step), device_id_type=MESH)
    pl.semaphore_signal(barrier, inc=1, device_id={"span": sibling}, device_id_type=MESH)
    for d in (1, 2, 3):
        pl.semaphore_signal(barrier, inc=1, device_id={"span": (span + 2 * d) % 8}, device_id_type=MESH)
        pl.semaphore_signal(barrier, inc=1, device_id={"mp": (y + d) % NY}, device_id_type=MESH)
    pl.semaphore_wait(barrier, 11)

    z_copy(kv_ref, 3, 3).start()
    z_copy(kv_ref, 4, -3).start()
    z_copy(kv_ref, 1, 1).start()
    z_copy(kv_ref, 2, -1).start()
    c_copy(kv_ref, 0).start()
    for d in (1, 2, 3):
        @pl.when(x >= d)
        def _():
            q_copy(d).start()

    kvbuf[0, 0] = kv_ref[...]
    qbuf[0] = q_ref[...]
    acc[...] = jnp.zeros_like(acc)
    stat[...] = jnp.zeros_like(stat)
    stat[:, 0:1, :] = jnp.full((NX, 1, ROWS), LOW, jnp.float32)
    query_clips = NX - x
    key_position = lax.broadcasted_iota(jnp.int32, (TOK, 1), 0)

    def attend(which, base, moves, first_query):
        count = len(moves)
        keys = count * TOK
        clip = 2 * x + (core if which == 0 else 1 - core)
        length = tok_ref[clip]
        limits = [length - TOK * ((z - r + 2 * NZ) % NZ) for r in moves]
        values = kvbuf[which, pl.ds(base, count), 1].reshape(keys, HD)
        vtbuf[:, 0:keys] = values.T

        def one_query(i, carry):
            key_rows = kvbuf[which, pl.ds(base, count), 0].reshape(keys, HD)
            query_rows = jnp.concatenate(
                [qbuf[i, :, h * HD:(h + 1) * HD] for h in range(GROUP)], axis=0
            )
            scores = lax.dot_general(
                key_rows, query_rows, (((1,), (1,)), ((), ())),
                preferred_element_type=jnp.float32,
            )
            scores = jnp.concatenate(
                [
                    jnp.where(key_position < limits[n], scores[n * TOK:(n + 1) * TOK], -jnp.inf)
                    for n in range(count)
                ],
                axis=0,
            )
            old_max = stat[i, 0:1, :]
            new_max = jnp.maximum(old_max, jnp.max(scores, axis=0, keepdims=True))
            weights = jnp.exp2((scores - new_max) * EXP_SCALE)
            shrink = jnp.exp2((old_max - new_max) * EXP_SCALE)
            stat[i, 0:1, :] = new_max
            stat[i, 1:2, :] = stat[i, 1:2, :] * shrink + jnp.sum(weights, axis=0, keepdims=True)
            acc[i] = acc[i] * shrink + jnp.dot(
                vtbuf[:, 0:keys], weights.astype(jnp.bfloat16), preferred_element_type=jnp.float32
            )
            return carry

        lax.fori_loop(first_query, query_clips, one_query, 0)

    def forward(slot, dst_slot, step):
        z_copy(kvbuf.at[0, slot], dst_slot, step).start()

    def arrived(slot):
        z_copy(kvbuf.at[0, slot], slot, 1).wait_recv()

    def to_sibling(slot):
        c_copy(kvbuf.at[0, slot], slot).start()

    def from_sibling(slot):
        c_copy(kvbuf.at[0, slot], slot).wait_recv()

    def centres(k, last):
        right, left = 6 * k - 3, 6 * k - 2
        arrived(right)
        if last is None:
            forward(right, right + 6, 3)
        else:
            @pl.when(jnp.logical_not(last))
            def _():
                forward(right, right + 6, 3)
        forward(right, 6 * k - 1, -1)
        forward(right, 6 * k, 1)
        to_sibling(right)
        arrived(left)
        forward(left, 6 * k + 1, 1)
        if last is None:
            forward(left, left + 6, -3)
            forward(left, 6 * k + 2, -1)
        else:
            @pl.when(jnp.logical_not(last))
            def _():
                forward(left, left + 6, -3)
                forward(left, 6 * k + 2, -1)
        to_sibling(left)

    sib_first = jnp.where(core == 1, 0, 1)

    for slot in (1, 2):
        arrived(slot)
        to_sibling(slot)
    centres(1, None)
    for d in (1, 2, 3):
        @pl.when(x + d < NX)
        def _():
            q_copy(d).wait_recv()
    attend(0, 0, (0, 1, -1, 3, -3), 0)
    for slot in range(5):
        from_sibling(slot)
    attend(1, 0, (0, 1, -1, 3, -3), sib_first)

    def round_of(k, carry):
        base = 6 * k - 7
        for n in range(4):
            arrived(base + n)
            to_sibling(base + n)
        centres(k, k == 5)
        moves = (3 * k - 4, 3 * k - 2, 4 - 3 * k, 2 - 3 * k, 3 * k, -3 * k)
        attend(0, base, moves, 0)
        for n in range(6):
            from_sibling(base + n)
        attend(1, base, moves, sib_first)
        return carry

    lax.fori_loop(2, 6, round_of, 0)

    for slot in (29, 30, 31):
        arrived(slot)
        to_sibling(slot)
    attend(0, 29, (14, 16, -14), 0)
    for slot in (29, 30, 31):
        from_sibling(slot)
    attend(1, 29, (14, 16, -14), sib_first)

    for d in (1, 2, 3):
        @pl.when(x + d < NX)
        def _():
            obuf[d] = acc[d].astype(jnp.bfloat16)
            sbuf[d] = stat[d]
            o_copy(d).start()
            s_copy(d).start()

    own_level = noise_ref[span]
    level = lax.broadcasted_iota(jnp.int32, (gate_ref.shape[0], 1), 0)
    gate_row = jnp.sum(
        jnp.where(level == own_level, gate_ref[...].astype(jnp.float32), 0.0), axis=0, keepdims=True
    )
    scale_row = gain_ref[...].astype(jnp.float32) * (1.0 + gate_row)

    for d in (1, 2, 3):
        @pl.when(x >= d)
        def _():
            s_copy(d).wait_recv()
            o_copy(d).wait_recv()
            old_max, part_max = stat[0, 0:1, :], srecv[d, 0:1, :]
            new_max = jnp.maximum(old_max, part_max)
            mine = jnp.exp2((old_max - new_max) * EXP_SCALE)
            other = jnp.exp2((part_max - new_max) * EXP_SCALE)
            stat[0, 0:1, :] = new_max
            stat[0, 1:2, :] = stat[0, 1:2, :] * mine + srecv[d, 1:2, :] * other
            acc[0] = acc[0] * mine + orecv[d].astype(jnp.float32) * other

    attended = acc[0] / stat[0, 1:2, :]
    acc[0] = attended
    column = jnp.sum(attended * attended, axis=0, keepdims=True)
    pair = column[:, 0:128] + column[:, 128:256] + column[:, 256:384]
    square = jnp.broadcast_to(pair, (8, 128))
    square = square + pltpu.roll(square, TOK, 1)
    sqsend[...] = square
    for d in (1, 2, 3):
        y_copy(d).start()
    for d in (1, 2, 3):
        y_copy(d).wait_recv()
    total = square + sqrecv[1] + sqrecv[2] + sqrecv[3]
    inverse = lax.rsqrt(total[0:1, :] / (HEADS * HD) + 1e-06)
    token = z * TOK + lax.broadcasted_iota(jnp.int32, (TOK, 1), 0)
    usable = token < tok_ref[span]
    for p in range(GROUP // 2):
        turned = (acc[0, :, p * 128:(p + 1) * 128] * inverse).T
        for half in range(2):
            h = 2 * p + half
            piece = turned[half * TOK:(half + 1) * TOK] * scale_row[:, h * HD:(h + 1) * HD]
            out_ref[:, h * HD:(h + 1) * HD] = jnp.where(usable, piece, 0.0).astype(jnp.bfloat16)

    def drain(slot, carry):
        z_copy(kvbuf.at[0, slot], slot, 1).wait_send()
        return carry

    lax.fori_loop(1, NZ, drain, 0)

    def drain_sibling(slot, carry):
        c_copy(kvbuf.at[0, slot], slot).wait_send()
        return carry

    lax.fori_loop(0, NZ, drain_sibling, 0)
    for d in (1, 2, 3):
        y_copy(d).wait_send()

        @pl.when(x >= d)
        def _():
            q_copy(d).wait_send()

        @pl.when(x + d < NX)
        def _():
            o_copy(d).wait_send()
            s_copy(d).wait_send()


def per_device(queries, keys_values, clip_tokens, noise_level, level_gate, out_gain):
    vmem = pl.BlockSpec(memory_space=pltpu.VMEM)
    smem = pl.BlockSpec(memory_space=pltpu.SMEM)
    dma = pltpu.SemaphoreType.DMA
    out = pl.pallas_call(
        kernel,
        out_shape=jax.ShapeDtypeStruct((TOK, GROUP * HD), jnp.bfloat16),
        in_specs=[smem, smem, vmem, vmem, vmem, vmem],
        out_specs=vmem,
        scratch_shapes=[
            pltpu.VMEM((2, NZ, 2, TOK, HD), jnp.bfloat16),
            pltpu.VMEM((HD, 6 * TOK), jnp.bfloat16),
            pltpu.VMEM((NX, TOK, GROUP * HD), jnp.bfloat16),
            pltpu.VMEM((NX, HD, ROWS), jnp.float32),
            pltpu.VMEM((NX, 8, ROWS), jnp.float32),
            pltpu.VMEM((NX, HD, ROWS), jnp.bfloat16),
            pltpu.VMEM((NX, 8, ROWS), jnp.float32),
            pltpu.VMEM((NX, HD, ROWS), jnp.bfloat16),
            pltpu.VMEM((NX, 8, ROWS), jnp.float32),
            pltpu.VMEM((8, 128), jnp.float32),
            pltpu.VMEM((NY, 8, 128), jnp.float32),
            dma((NZ,)), dma((NZ,)), dma((NZ,)), dma((NZ,)),
            dma((NX,)), dma((NX,)), dma((NX,)), dma((NX,)),
            dma((NX,)), dma((NX,)), dma((NY,)), dma((NY,)),
        ],
        compiler_params=pltpu.CompilerParams(collective_id=0, has_side_effects=True),
        name="clip_attention",
    )(
        clip_tokens,
        noise_level,
        queries[0],
        keys_values[:, 0],
        level_gate,
        out_gain.reshape(1, GROUP * HD),
    )
    return out[None]


def solution(mesh):
    placed = (
        P("span", "seq", "mp"),
        P(None, "span", "seq", "mp"),
        P(),
        P(),
        P(None, "mp"),
        P("mp"),
    )
    return jax.shard_map(
        per_device, mesh=mesh, in_specs=placed, out_specs=P("span", "seq", "mp"), check_vma=False
    )
```

time: 388 us -> 71.9 us (0.19)
  the two profiles are of different devices: /device:TPU:6 before, /device:TPU:4 now
where the time goes in v1:
time: 71.9 us; the launch traced here: 71.7 us
  Pallas kernels  68.9 us (96%)
  local copies, waits for them, and re-layouts  2.8 us (4%)
    pallas_call x1, Pallas kernels, per_device(): pl.pallas_call(kernel, out_shape=jax.ShapeDtypeStruct((TOK, GROUP * HD),...  68.9 us
    unnamed x3, local copies, waits for them, and re-layouts  2.22 us

profile of v1, /device:TPU:4, one launch (start us, length us, event | category | flops | bytes accessed | tf_op | source)
XLA Modules:
  0.0 71.7 jit_solution(5709404221841101694)
XLA Ops:
  0.0 0.0 copy-start
  0.0 0.7 copy-done
  0.7 0.6 reshape.3.gain_ref
  1.3 68.9 %clip_attention.1 = bf16[64,768]{1,0:T(8,128)(2,1)} custom-call(s32[8]{0:T(128)} %tok_ref.1, s32[8]{0:T(128)} %noise_ref.1, bf16[64,768]{1,0:T(8,128)(2,1)} %bitcast.4, bf16[2,64,128]{2,1,0:T(8,128)(2,1)} %bitcast.5, bf16[64,768]{1,0:T(8,128)(2,1)} %gate_ref.1, bf16[1,768]{1,0:T(2,128)(2,1)} %reshape.3.gain_ref), custom_call_target="tpu_custom_call" | custom-call | tf_op jit(solution)/shard_map/clip_attention/pallas_call | solution.py:299
  70.1 1.5 %copy.8 = bf16[1,64,768]{2,1,0:T(8,128)(2,1)} copy(bf16[1,64,768]{2,1,0:T(8,128)(2,1)} %bitcast.3) | data formatting | bytes 196608
Async XLA Ops:
  0.0 0.7 copy-start

commit v2 on v1

--- a/solution.py
+++ b/solution.py
@@ -23,7 +23,8 @@
 
 
 def kernel(
-    tok_ref, noise_ref, q_ref, kv_ref, gate_ref, gain_ref, out_ref,
+    tok_hbm, noise_hbm, q_hbm, kv_hbm, gate_hbm, gain_hbm, out_ref,
+    tok_ref, noise_ref, gate_ref, gain_ref, in_sem,
     kvbuf, vtbuf, qbuf, acc, stat, obuf, sbuf, orecv, srecv, sqsend, sqrecv,
     z_send, z_recv, c_send, c_recv, q_send, q_recv, o_send, o_recv, s_send, s_recv, y_send, y_recv,
 ):
@@ -44,6 +45,13 @@
             device_id=along_z(step), device_id_type=MESH,
         )
 
+    def both_copy(src, dst_slot, step):
+        return pltpu.make_async_remote_copy(
+            src_ref=src, dst_ref=kvbuf.at[1, dst_slot],
+            send_sem=c_send.at[dst_slot], recv_sem=c_recv.at[dst_slot],
+            device_id={"span": sibling, "seq": (z + step + NZ) % NZ}, device_id_type=MESH,
+        )
+
     def c_copy(src, slot):
         return pltpu.make_async_remote_copy(
             src_ref=src, dst_ref=kvbuf.at[1, slot],
@@ -53,7 +61,7 @@
 
     def q_copy(d):
         return pltpu.make_async_remote_copy(
-            src_ref=q_ref, dst_ref=qbuf.at[d],
+            src_ref=qbuf.at[0], dst_ref=qbuf.at[d],
             send_sem=q_send.at[d], recv_sem=q_recv.at[d],
             device_id={"span": (span - 2 * d + 8) % 8}, device_id_type=MESH,
         )
@@ -79,43 +87,60 @@
             device_id={"mp": (y + d) % NY}, device_id_type=MESH,
         )
 
+    loads = [
+        pltpu.make_async_copy(src, dst, in_sem.at[n])
+        for n, (src, dst) in enumerate(
+            (
+                (kv_hbm, kvbuf.at[0, 0]), (q_hbm, qbuf.at[0]), (gate_hbm, gate_ref),
+                (gain_hbm, gain_ref), (tok_hbm, tok_ref), (noise_hbm, noise_ref),
+            )
+        )
+    ]
     barrier = pltpu.get_barrier_semaphore()
+    for load in loads:
+        load.start()
     for step in (1, -1, 3, -3):
         pl.semaphore_signal(barrier, inc=1, device_id=along_z(step), device_id_type=MESH)
     pl.semaphore_signal(barrier, inc=1, device_id={"span": sibling}, device_id_type=MESH)
     for d in (1, 2, 3):
         pl.semaphore_signal(barrier, inc=1, device_id={"span": (span + 2 * d) % 8}, device_id_type=MESH)
         pl.semaphore_signal(barrier, inc=1, device_id={"mp": (y + d) % NY}, device_id_type=MESH)
-    pl.semaphore_wait(barrier, 11)
-
-    z_copy(kv_ref, 3, 3).start()
-    z_copy(kv_ref, 4, -3).start()
-    z_copy(kv_ref, 1, 1).start()
-    z_copy(kv_ref, 2, -1).start()
-    c_copy(kv_ref, 0).start()
-    for d in (1, 2, 3):
-        @pl.when(x >= d)
-        def _():
-            q_copy(d).start()
-
-    kvbuf[0, 0] = kv_ref[...]
-    qbuf[0] = q_ref[...]
+    for step in (1, -1):
+        pl.semaphore_signal(
+            barrier, inc=1, device_id={"span": sibling, "seq": (z + step + NZ) % NZ}, device_id_type=MESH
+        )
     acc[...] = jnp.zeros_like(acc)
     stat[...] = jnp.zeros_like(stat)
     stat[:, 0:1, :] = jnp.full((NX, 1, ROWS), LOW, jnp.float32)
+    loads[0].wait()
+    pl.semaphore_wait(barrier, 13)
+
+    own = kvbuf.at[0, 0]
+    z_copy(own, 3, 3).start()
+    z_copy(own, 4, -3).start()
+    z_copy(own, 1, 1).start()
+    z_copy(own, 2, -1).start()
+    c_copy(own, 0).start()
+    loads[1].wait()
+    loads[4].wait()
+    for d in (1, 2, 3):
+        @pl.when(x >= d)
+        def _():
+            q_copy(d).start()
+
     query_clips = NX - x
     key_position = lax.broadcasted_iota(jnp.int32, (TOK, 1), 0)
 
-    def attend(which, base, moves, first_query):
+    def attend(which, base, moves, queries):
         count = len(moves)
         keys = count * TOK
         clip = 2 * x + (core if which == 0 else 1 - core)
         length = tok_ref[clip]
         limits = [length - TOK * ((z - r + 2 * NZ) % NZ) for r in moves]
         values = kvbuf[which, pl.ds(base, count), 1].reshape(keys, HD)
-        vtbuf[:, 0:keys] = values.T
-
-        def one_query(i, carry):
+        vtbuf[which, :, 0:keys] = values.T
+
+        def one_query(i):
             key_rows = kvbuf[which, pl.ds(base, count), 0].reshape(keys, HD)
             query_rows = jnp.concatenate(
                 [qbuf[i, :, h * HD:(h + 1) * HD] for h in range(GROUP)], axis=0
@@ -138,14 +163,24 @@
             stat[i, 0:1, :] = new_max
             stat[i, 1:2, :] = stat[i, 1:2, :] * shrink + jnp.sum(weights, axis=0, keepdims=True)
             acc[i] = acc[i] * shrink + jnp.dot(
-                vtbuf[:, 0:keys], weights.astype(jnp.bfloat16), preferred_element_type=jnp.float32
+                vtbuf[which, :, 0:keys], weights.astype(jnp.bfloat16), preferred_element_type=jnp.float32
             )
+
+        if queries is None:
+            return one_query
+
+        def step(i, carry):
+            one_query(i)
             return carry
 
-        lax.fori_loop(first_query, query_clips, one_query, 0)
+        lax.fori_loop(queries, query_clips, step, 0)
 
     def forward(slot, dst_slot, step):
         z_copy(kvbuf.at[0, slot], dst_slot, step).start()
+
+    def forward_both(slot, dst_slot, step):
+        forward(slot, dst_slot, step)
+        both_copy(kvbuf.at[0, slot], dst_slot, step).start()
 
     def arrived(slot):
         z_copy(kvbuf.at[0, slot], slot, 1).wait_recv()
@@ -161,26 +196,49 @@
         arrived(right)
         if last is None:
             forward(right, right + 6, 3)
+            arrived(left)
+            forward(left, left + 6, -3)
+            forward(right, 6 * k, 1)
+            forward(right, 6 * k - 1, -1)
+            forward(left, 6 * k + 2, -1)
+            forward(left, 6 * k + 1, 1)
         else:
+            @pl.when(last)
+            def _():
+                forward_both(right, 6 * k, 1)
+                forward_both(right, 6 * k - 1, -1)
+
             @pl.when(jnp.logical_not(last))
             def _():
                 forward(right, right + 6, 3)
-        forward(right, 6 * k - 1, -1)
-        forward(right, 6 * k, 1)
-        to_sibling(right)
-        arrived(left)
-        forward(left, 6 * k + 1, 1)
-        if last is None:
-            forward(left, left + 6, -3)
-            forward(left, 6 * k + 2, -1)
-        else:
+
+            arrived(left)
+
+            @pl.when(last)
+            def _():
+                forward_both(left, 6 * k + 1, 1)
+
             @pl.when(jnp.logical_not(last))
             def _():
                 forward(left, left + 6, -3)
+                forward(right, 6 * k, 1)
+                forward(right, 6 * k - 1, -1)
                 forward(left, 6 * k + 2, -1)
+                forward(left, 6 * k + 1, 1)
+
+        to_sibling(right)
         to_sibling(left)
 
+    def leaves(base):
+        for n in range(4):
+            arrived(base + n)
+            to_sibling(base + n)
+
+    def moves_of(k):
+        return (3 * k - 4, 3 * k - 2, 4 - 3 * k, 2 - 3 * k, 3 * k, -3 * k)
+
     sib_first = jnp.where(core == 1, 0, 1)
+    first_moves = (0, 1, -1, 3, -3)
 
     for slot in (1, 2):
         arrived(slot)
@@ -190,48 +248,60 @@
         @pl.when(x + d < NX)
         def _():
             q_copy(d).wait_recv()
-    attend(0, 0, (0, 1, -1, 3, -3), 0)
+    attend(0, 0, first_moves, 0)
+    leaves(5)
+    centres(2, None)
     for slot in range(5):
         from_sibling(slot)
-    attend(1, 0, (0, 1, -1, 3, -3), sib_first)
+    attend(1, 0, first_moves, sib_first)
+    attend(0, 5, moves_of(2), 0)
 
     def round_of(k, carry):
         base = 6 * k - 7
-        for n in range(4):
-            arrived(base + n)
-            to_sibling(base + n)
+        leaves(base)
         centres(k, k == 5)
-        moves = (3 * k - 4, 3 * k - 2, 4 - 3 * k, 2 - 3 * k, 3 * k, -3 * k)
-        attend(0, base, moves, 0)
         for n in range(6):
-            from_sibling(base + n)
-        attend(1, base, moves, sib_first)
+            from_sibling(base - 6 + n)
+        attend(1, base - 6, moves_of(k - 1), sib_first)
+        attend(0, base, moves_of(k), 0)
         return carry
 
-    lax.fori_loop(2, 6, round_of, 0)
+    lax.fori_loop(3, 6, round_of, 0)
+    for n in range(6):
+        from_sibling(23 + n)
+    attend(1, 23, moves_of(5), sib_first)
 
     for slot in (29, 30, 31):
         arrived(slot)
-        to_sibling(slot)
-    attend(0, 29, (14, 16, -14), 0)
+    mine = attend(0, 29, (14, 16, -14), None)
     for slot in (29, 30, 31):
         from_sibling(slot)
-    attend(1, 29, (14, 16, -14), sib_first)
-
-    for d in (1, 2, 3):
+    other = attend(1, 29, (14, 16, -14), None)
+
+    for d in (2, 3, 1):
         @pl.when(x + d < NX)
         def _():
+            mine(d)
+            other(d)
             obuf[d] = acc[d].astype(jnp.bfloat16)
             sbuf[d] = stat[d]
             o_copy(d).start()
             s_copy(d).start()
-
+    mine(0)
+
+    @pl.when(core == 1)
+    def _():
+        other(0)
+
+    loads[2].wait()
+    loads[3].wait()
+    loads[5].wait()
     own_level = noise_ref[span]
     level = lax.broadcasted_iota(jnp.int32, (gate_ref.shape[0], 1), 0)
     gate_row = jnp.sum(
         jnp.where(level == own_level, gate_ref[...].astype(jnp.float32), 0.0), axis=0, keepdims=True
     )
-    scale_row = gain_ref[...].astype(jnp.float32) * (1.0 + gate_row)
+    scale_row = gain_ref[...].astype(jnp.float32).reshape(1, GROUP * HD) * (1.0 + gate_row)
 
     for d in (1, 2, 3):
         @pl.when(x >= d)
@@ -253,7 +323,7 @@
     square = jnp.broadcast_to(pair, (8, 128))
     square = square + pltpu.roll(square, TOK, 1)
     sqsend[...] = square
-    for d in (1, 2, 3):
+    for d in (2, 1, 3):
         y_copy(d).start()
     for d in (1, 2, 3):
         y_copy(d).wait_recv()
@@ -294,16 +364,21 @@
 
 def per_device(queries, keys_values, clip_tokens, noise_level, level_gate, out_gain):
     vmem = pl.BlockSpec(memory_space=pltpu.VMEM)
-    smem = pl.BlockSpec(memory_space=pltpu.SMEM)
+    hbm = pl.BlockSpec(memory_space=pltpu.HBM)
     dma = pltpu.SemaphoreType.DMA
     out = pl.pallas_call(
         kernel,
         out_shape=jax.ShapeDtypeStruct((TOK, GROUP * HD), jnp.bfloat16),
-        in_specs=[smem, smem, vmem, vmem, vmem, vmem],
+        in_specs=[hbm] * 6,
         out_specs=vmem,
         scratch_shapes=[
+            pltpu.SMEM(clip_tokens.shape, jnp.int32),
+            pltpu.SMEM(noise_level.shape, jnp.int32),
+            pltpu.VMEM(level_gate.shape, jnp.bfloat16),
+            pltpu.VMEM(out_gain.shape, jnp.bfloat16),
+            dma((6,)),
             pltpu.VMEM((2, NZ, 2, TOK, HD), jnp.bfloat16),
-            pltpu.VMEM((HD, 6 * TOK), jnp.bfloat16),
+            pltpu.VMEM((2, HD, 6 * TOK), jnp.bfloat16),
             pltpu.VMEM((NX, TOK, GROUP * HD), jnp.bfloat16),
             pltpu.VMEM((NX, HD, ROWS), jnp.float32),
             pltpu.VMEM((NX, 8, ROWS), jnp.float32),
@@ -317,15 +392,13 @@
             dma((NX,)), dma((NX,)), dma((NX,)), dma((NX,)),
             dma((NX,)), dma((NX,)), dma((NY,)), dma((NY,)),
         ],
-        compiler_params=pltpu.CompilerParams(collective_id=0, has_side_effects=True),
+        compiler_params=pltpu.CompilerParams(collective_id=0, has_side_effects=True, vmem_limit_bytes=32 * 2**20),
         name="clip_attention",
     )(
-        clip_tokens,
-        noise_level,
-        queries[0],
-        keys_values[:, 0],
-        level_gate,
-        out_gain.reshape(1, GROUP * HD),
+        *(
+            pltpu.with_memory_space_constraint(a, pltpu.HBM)
+            for a in (clip_tokens, noise_level, queries[0], keys_values[:, 0], level_gate, out_gain)
+        ),
     )
     return out[None]
 

time: 71.9 us -> 64.8 us (0.901)
  the two profiles are of different devices: /device:TPU:4 before, /device:TPU:6 now
where the time goes in v2:
time: 64.8 us; the launch traced here: 64.7 us
  Pallas kernels  64 us (99%)
    pallas_call x1, Pallas kernels, per_device(): pl.pallas_call(kernel, out_shape=jax.ShapeDtypeStruct((TOK, GROUP * HD),...  64 us

profile of v2, /device:TPU:6, one launch (start us, length us, event | category | flops | bytes accessed | tf_op | source)
XLA Modules:
  0.0 64.7 jit_solution(14537129789842088845)
XLA Ops:
  0.0 64.0 %clip_attention.1 = bf16[64,768]{1,0:T(8,128)(2,1)S(1)} custom-call(s32[8]{0:T(128)} %tok_hbm.1, s32[8]{0:T(128)} %noise_hbm.1, bf16[64,768]{1,0:T(8,128)(2,1)} %bitcast.4, bf16[2,64,128]{2,1,0:T(8,128)(2,1)} %bitcast.5, bf16[64,768]{1,0:T(8,128)(2,1)} %gate_hbm.1, bf16[768]{0:T(1024)(128)(2,1)} %gain_hbm.1), custom_call_target="tpu_custom_call" | custom-call | tf_op jit(solution)/shard_map/clip_attention/pallas_call | solution.py:369
  64.0 0.6 copy.8

commit v3 on v2

--- a/solution.py
+++ b/solution.py
@@ -131,28 +131,38 @@
     query_clips = NX - x
     key_position = lax.broadcasted_iota(jnp.int32, (TOK, 1), 0)
 
-    def attend(which, base, moves, queries):
-        count = len(moves)
-        keys = count * TOK
-        clip = 2 * x + (core if which == 0 else 1 - core)
-        length = tok_ref[clip]
-        limits = [length - TOK * ((z - r + 2 * NZ) % NZ) for r in moves]
-        values = kvbuf[which, pl.ds(base, count), 1].reshape(keys, HD)
-        vtbuf[which, :, 0:keys] = values.T
+    def attend(parts, queries):
+        keys = sum(len(moves) for _, _, moves in parts) * TOK
+
+        def rows_of(kind):
+            return jnp.concatenate(
+                [kvbuf[which, pl.ds(base, len(moves)), kind].reshape(-1, HD) for which, base, moves in parts],
+                axis=0,
+            )
+
+        vtbuf[:, 0:keys] = rows_of(1).T
+        limits = []
+        for which, _, moves in parts:
+            length = tok_ref[2 * x + (core if which == 0 else 1 - core)]
+            limits += [(which, length - TOK * ((z - r + 2 * NZ) % NZ)) for r in moves]
 
         def one_query(i):
-            key_rows = kvbuf[which, pl.ds(base, count), 0].reshape(keys, HD)
+            later_clip = (i == 0) & (core == 0)
             query_rows = jnp.concatenate(
                 [qbuf[i, :, h * HD:(h + 1) * HD] for h in range(GROUP)], axis=0
             )
             scores = lax.dot_general(
-                key_rows, query_rows, (((1,), (1,)), ((), ())),
+                rows_of(0), query_rows, (((1,), (1,)), ((), ())),
                 preferred_element_type=jnp.float32,
             )
             scores = jnp.concatenate(
                 [
-                    jnp.where(key_position < limits[n], scores[n * TOK:(n + 1) * TOK], -jnp.inf)
-                    for n in range(count)
+                    jnp.where(
+                        key_position < (jnp.where(later_clip, 0, limit) if which else limit),
+                        scores[n * TOK:(n + 1) * TOK],
+                        -jnp.inf,
+                    )
+                    for n, (which, limit) in enumerate(limits)
                 ],
                 axis=0,
             )
@@ -163,7 +173,7 @@
             stat[i, 0:1, :] = new_max
             stat[i, 1:2, :] = stat[i, 1:2, :] * shrink + jnp.sum(weights, axis=0, keepdims=True)
             acc[i] = acc[i] * shrink + jnp.dot(
-                vtbuf[which, :, 0:keys], weights.astype(jnp.bfloat16), preferred_element_type=jnp.float32
+                vtbuf[:, 0:keys], weights.astype(jnp.bfloat16), preferred_element_type=jnp.float32
             )
 
         if queries is None:
@@ -194,7 +204,12 @@
     def centres(k, last):
         right, left = 6 * k - 3, 6 * k - 2
         arrived(right)
-        if last is None:
+        if last:
+            forward_both(right, 6 * k, 1)
+            forward_both(right, 6 * k - 1, -1)
+            arrived(left)
+            forward_both(left, 6 * k + 1, 1)
+        else:
             forward(right, right + 6, 3)
             arrived(left)
             forward(left, left + 6, -3)
@@ -202,30 +217,6 @@
             forward(right, 6 * k - 1, -1)
             forward(left, 6 * k + 2, -1)
             forward(left, 6 * k + 1, 1)
-        else:
-            @pl.when(last)
-            def _():
-                forward_both(right, 6 * k, 1)
-                forward_both(right, 6 * k - 1, -1)
-
-            @pl.when(jnp.logical_not(last))
-            def _():
-                forward(right, right + 6, 3)
-
-            arrived(left)
-
-            @pl.when(last)
-            def _():
-                forward_both(left, 6 * k + 1, 1)
-
-            @pl.when(jnp.logical_not(last))
-            def _():
-                forward(left, left + 6, -3)
-                forward(right, 6 * k, 1)
-                forward(right, 6 * k - 1, -1)
-                forward(left, 6 * k + 2, -1)
-                forward(left, 6 * k + 1, 1)
-
         to_sibling(right)
         to_sibling(left)
 
@@ -237,61 +228,55 @@
     def moves_of(k):
         return (3 * k - 4, 3 * k - 2, 4 - 3 * k, 2 - 3 * k, 3 * k, -3 * k)
 
-    sib_first = jnp.where(core == 1, 0, 1)
     first_moves = (0, 1, -1, 3, -3)
-
+    last_moves = (14, 16, -14)
+
+    centres(1, False)
     for slot in (1, 2):
         arrived(slot)
         to_sibling(slot)
-    centres(1, None)
     for d in (1, 2, 3):
         @pl.when(x + d < NX)
         def _():
             q_copy(d).wait_recv()
-    attend(0, 0, first_moves, 0)
+    attend(((0, 0, first_moves),), 0)
+    centres(2, False)
     leaves(5)
-    centres(2, None)
     for slot in range(5):
         from_sibling(slot)
-    attend(1, 0, first_moves, sib_first)
-    attend(0, 5, moves_of(2), 0)
+    attend(((1, 0, first_moves), (0, 5, moves_of(2))), 0)
 
     def round_of(k, carry):
         base = 6 * k - 7
+        centres(k, False)
         leaves(base)
-        centres(k, k == 5)
         for n in range(6):
             from_sibling(base - 6 + n)
-        attend(1, base - 6, moves_of(k - 1), sib_first)
-        attend(0, base, moves_of(k), 0)
+        attend(((1, base - 6, moves_of(k - 1)), (0, base, moves_of(k))), 0)
         return carry
 
-    lax.fori_loop(3, 6, round_of, 0)
+    lax.fori_loop(3, 5, round_of, 0)
+    centres(5, True)
+    leaves(23)
     for n in range(6):
-        from_sibling(23 + n)
-    attend(1, 23, moves_of(5), sib_first)
+        from_sibling(17 + n)
+    attend(((1, 17, moves_of(4)), (0, 23, moves_of(5))), 0)
 
     for slot in (29, 30, 31):
         arrived(slot)
-    mine = attend(0, 29, (14, 16, -14), None)
-    for slot in (29, 30, 31):
+    for slot in range(23, 32):
         from_sibling(slot)
-    other = attend(1, 29, (14, 16, -14), None)
-
-    for d in (2, 3, 1):
+    late = attend(((1, 23, moves_of(5)), (0, 29, last_moves), (1, 29, last_moves)), None)
+
+    for d in (2, 1, 3):
         @pl.when(x + d < NX)
         def _():
-            mine(d)
-            other(d)
+            late(d)
             obuf[d] = acc[d].astype(jnp.bfloat16)
             sbuf[d] = stat[d]
             o_copy(d).start()
             s_copy(d).start()
-    mine(0)
-
-    @pl.when(core == 1)
-    def _():
-        other(0)
+    late(0)
 
     loads[2].wait()
     loads[3].wait()
@@ -378,7 +363,7 @@
             pltpu.VMEM(out_gain.shape, jnp.bfloat16),
             dma((6,)),
             pltpu.VMEM((2, NZ, 2, TOK, HD), jnp.bfloat16),
-            pltpu.VMEM((2, HD, 6 * TOK), jnp.bfloat16),
+            pltpu.VMEM((HD, 12 * TOK), jnp.bfloat16),
             pltpu.VMEM((NX, TOK, GROUP * HD), jnp.bfloat16),
             pltpu.VMEM((NX, HD, ROWS), jnp.float32),
             pltpu.VMEM((NX, 8, ROWS), jnp.float32),

time: 64.8 us -> 62.7 us (0.968)
  Pallas kernels: 64 us -> 61.4 us
    pallas_call x1, Pallas kernels: 64 us -> 61.4 us  [per_device(): pl.pallas_call(kernel, out_shape=jax.ShapeDtypeStruct((TOK, GROUP * HD),...]
where the time goes in v3:
time: 62.7 us; the launch traced here: 62 us
  Pallas kernels  61.4 us (98%)
  local copies, waits for them, and re-layouts  0.64 us (1%)
    pallas_call x1, Pallas kernels, per_device(): pl.pallas_call(kernel, out_shape=jax.ShapeDtypeStruct((TOK, GROUP * HD),...  61.4 us

profile of v3, /device:TPU:6, one launch (start us, length us, event | category | flops | bytes accessed | tf_op | source)
XLA Modules:
  0.0 62.0 jit_solution(16621710604540148161)
XLA Ops:
  0.0 61.4 %clip_attention.1 = bf16[64,768]{1,0:T(8,128)(2,1)S(1)} custom-call(s32[8]{0:T(128)} %tok_hbm.1, s32[8]{0:T(128)} %noise_hbm.1, bf16[64,768]{1,0:T(8,128)(2,1)} %bitcast.4, bf16[2,64,128]{2,1,0:T(8,128)(2,1)} %bitcast.5, bf16[64,768]{1,0:T(8,128)(2,1)} %gate_hbm.1, bf16[768]{0:T(1024)(128)(2,1)} %gain_hbm.1), custom_call_target="tpu_custom_call" | custom-call | tf_op jit(solution)/shard_map/clip_attention/pallas_call | solution.py:354
  61.4 0.6 %copy.8 = bf16[1,64,768]{2,1,0:T(8,128)(2,1)} copy(bf16[1,64,768]{2,1,0:T(8,128)(2,1)S(1)} %bitcast.3) | data formatting | bytes 196608
